TPU v7x, 32 devices: a whole 2x2x4 slice. The times are simulated.
32 devices in a mesh: brow: 4 (over z), bcol: 8 (over y, x, core).
Axes of the slice: x: 2, y: 2, z: 4, core: 2. Of those that a mesh axis runs over, the one named last changes fastest.
Arguments:
- anc_tiles: int32 [1, 12], replicated, may hold values from 0 to 31, as said below
- ancestor_inverse: float32 [16384, 16384], P('brow', 'bcol'), as said below
- factor_pieces: float32 [16384, 1536], P('bcol', 'brow'), may hold values from -6 to 6
Outputs:
- inverse_rows: float32 [1536, 16384], P('bcol', 'brow')
Inputs may be any that keep to these rules, and one draw needn't show every extreme that they name: `anc_tiles`: each row lists 12 different tiles; tile 32 - 1 is listed in every row, tile 0 in row 0. ancestor_inverse is symmetric.
All inputs are finite; a program needn't handle non-finite values.
Results may differ from a plain program's by a relative error of at most 0.00007.
Values sent between devices are 32-bit elements; how exact they have to be, the bound alone decides.
A program may use at most 128 MiB of HBM per device.

v0:
```python
import jax
import jax.numpy as jnp
from jax import lax
from jax.sharding import PartitionSpec as P

TS = 512
W = 1536
A = 32
K = 1
CHUNKS = 4


def split(x):
    high = lax.reduce_precision(x, exponent_bits=8, mantissa_bits=7)
    return (high.astype(jnp.bfloat16), (x - high).astype(jnp.bfloat16))


def product(x, y, **kwargs):
    return lax.dot_general(
        x, y, (((1,), (1,)), ((), ())), preferred_element_type=jnp.float32, **kwargs
    )


def local(anc_tiles, ancestor_inverse, factor_pieces):
    col_index = lax.axis_index("bcol")
    row_index = lax.axis_index("brow")
    n_col = lax.axis_size("bcol")
    n_row = lax.axis_size("brow")
    block_rows, block_cols = ancestor_inverse.shape
    tiles_col, tiles_row = (block_cols // TS, block_rows // TS)
    total_cols = factor_pieces.shape[1] * n_row
    tile_ids = jnp.arange(A, dtype=jnp.int32)
    listed = jnp.any(anc_tiles[:, :, None] == tile_ids[None, None, :], axis=1)
    col_super = (row_index * factor_pieces.shape[1] + jnp.arange(factor_pieces.shape[1])) // W
    listed_col = lax.dynamic_slice_in_dim(listed, col_index * tiles_col, tiles_col, 1)
    col_mask = jnp.repeat(listed_col[col_super], TS, axis=1)
    factor = jnp.where(col_mask, factor_pieces.T, 0.0)
    width = total_cols // n_col // CHUNKS
    factor = factor.reshape(-1, CHUNKS, width, block_cols)
    gathered = [
        lax.all_gather(factor[:, q], "brow", axis=0, tiled=True).reshape(-1, block_cols)
        for q in range(CHUNKS)
    ]
    sums = []
    for q in range(CHUNKS):
        part = product(gathered[q], ancestor_inverse, precision=lax.Precision.HIGH)
        sums.append(lax.psum_scatter(part, "bcol", scatter_dimension=0, tiled=True))
    summed = jnp.concatenate(sums, axis=0)
    out_rows = summed.shape[0]
    row_super = (col_index * out_rows + jnp.arange(out_rows)) // W
    listed_row = lax.dynamic_slice_in_dim(listed, row_index * tiles_row, tiles_row, 1)
    out_mask = jnp.repeat(listed_row[row_super], TS, axis=1)
    return jnp.where(out_mask, -summed, 0.0)


def solution(mesh):
    in_specs = (P(), P("brow", "bcol"), P("bcol", "brow"))
    out_specs = P("bcol", "brow")
    return jax.shard_map(local, mesh=mesh, in_specs=in_specs, out_specs=out_specs, check_vma=False)
```

profile of v0, /device:TPU:0, one launch (start us, length us, event | category | flops | bytes accessed | tf_op | source)
XLA Modules:
  0.0 543.0 jit_solution(9109065422733536276)
XLA Ops:
  6.5 0.7 fusion.1
  7.4 0.5 broadcast_in_dim.19
  7.8 1.3 copy.8
  9.2 2.4 copy.6
  11.6 1.6 bitcast_select_fusion
  13.2 1.8 fusion.2
  15.0 0.7 all-gather.9.cloned.1.call-update
  15.8 0.7 all-gather.11.cloned.1.call-update
  16.5 0.5 all-gather.13.cloned.1.call-update
  17.1 64.2 %all-gather.15.cloned.1.call-done = f32[8,1,48,2048]{3,2,1,0:T(8,128)} async-done(((f32[2,1,48,2048]{3,2,1,0:T(8,128)}), f32[8,1,48,2048]{3,2,1,0:T(8,128)}) %all-gather.15.cloned.1.call-update) | async-done | bytes 3145744 | tf_op jit(solution)/shard_map/all_gather | solution.py:41
  81.4 26.1 %fusion.6 = f32[384,4096]{1,0:T(8,128)} fusion(f32[384,2048]{1,0:T(8,128)} %bitcast.24, f32[4096,2048]{1,0:T(8,128)} %param.4), kind=kOutput, calls=%fused_computation.9 | convolution fusion | flops 19327352832 | bytes 42991616 | tf_op jit(solution)/shard_map/dot_general | solution.py:19
  107.7 37.4 %all-gather.9.cloned.1.call-done = f32[8,1,48,2048]{3,2,1,0:T(8,128)} async-done(((f32[2,1,48,2048]{3,2,1,0:T(8,128)}), f32[8,1,48,2048]{3,2,1,0:T(8,128)}) %all-gather.9.cloned.1.call-update) | async-done | bytes 3145744 | tf_op jit(solution)/shard_map/all_gather | solution.py:41
  145.1 26.1 %fusion.3 = f32[384,4096]{1,0:T(8,128)} fusion(f32[384,2048]{1,0:T(8,128)} %bitcast.23, f32[4096,2048]{1,0:T(8,128)} %param.4), kind=kOutput, calls=%fused_computation.6 | convolution fusion | flops 19327352832 | bytes 42991616 | tf_op jit(solution)/shard_map/dot_general | solution.py:19
  171.3 37.5 %all-gather.11.cloned.1.call-done = f32[8,1,48,2048]{3,2,1,0:T(8,128)} async-done(((f32[2,1,48,2048]{3,2,1,0:T(8,128)}), f32[8,1,48,2048]{3,2,1,0:T(8,128)}) %all-gather.11.cloned.1.call-update) | async-done | bytes 3145744 | tf_op jit(solution)/shard_map/all_gather | solution.py:41
  208.9 26.1 %fusion.4 = f32[384,4096]{1,0:T(8,128)} fusion(f32[384,2048]{1,0:T(8,128)} %bitcast.22, f32[4096,2048]{1,0:T(8,128)} %param.4), kind=kOutput, calls=%fused_computation.7 | convolution fusion | flops 19327352832 | bytes 42991616 | tf_op jit(solution)/shard_map/dot_general | solution.py:19
  235.3 37.2 %all-gather.13.cloned.1.call-done = f32[8,1,48,2048]{3,2,1,0:T(8,128)} async-done(((f32[2,1,48,2048]{3,2,1,0:T(8,128)}), f32[8,1,48,2048]{3,2,1,0:T(8,128)}) %all-gather.13.cloned.1.call-update) | async-done | bytes 3145744 | tf_op jit(solution)/shard_map/all_gather | solution.py:41
  272.5 26.1 %fusion.5 = f32[384,4096]{1,0:T(8,128)} fusion(f32[384,2048]{1,0:T(8,128)} %bitcast.21, f32[4096,2048]{1,0:T(8,128)} %param.4), kind=kOutput, calls=%fused_computation.8 | convolution fusion | flops 19327352832 | bytes 42991616 | tf_op jit(solution)/shard_map/dot_general | solution.py:19
  298.7 0.3 broadcast_in_dim.18
  299.0 0.5 copy.7
  299.5 36.6 %reduce-scatter.11.cloned.1.call-done = f32[48,4096]{1,0:T(8,128)} async-done(((f32[384,4096]{1,0:T(8,128)}), f32[48,4096]{1,0:T(8,128)}) %reduce-scatter.11.cloned.1.call-update) | async-done | bytes 786448 | tf_op jit(solution)/shard_map/reduce_scatter | solution.py:47
  336.1 65.4 %reduce-scatter.5.cloned.1.call-done = f32[48,4096]{1,0:T(8,128)} async-done(((f32[384,4096]{1,0:T(8,128)}), f32[48,4096]{1,0:T(8,128)}) %reduce-scatter.5.cloned.1.call-update) | async-done | bytes 786448 | tf_op jit(solution)/shard_map/reduce_scatter | solution.py:47
  401.5 65.2 %reduce-scatter.7.cloned.1.call-done = f32[48,4096]{1,0:T(8,128)} async-done(((f32[384,4096]{1,0:T(8,128)}), f32[48,4096]{1,0:T(8,128)}) %reduce-scatter.7.cloned.1.call-update) | async-done | bytes 786448 | tf_op jit(solution)/shard_map/reduce_scatter | solution.py:47
  466.7 65.5 %reduce-scatter.9.cloned.1.call-done = f32[48,4096]{1,0:T(8,128)} async-done(((f32[384,4096]{1,0:T(8,128)}), f32[48,4096]{1,0:T(8,128)}) %reduce-scatter.9.cloned.1.call-update) | async-done | bytes 786448 | tf_op jit(solution)/shard_map/reduce_scatter | solution.py:47
  532.2 4.0 fusion
  (15 shorter events, 0.9 us)
Async XLA Ops:
  6.5 74.8 %all-gather.15.cloned.1.call-start = ((), (), s32[]{:S(2)}) async-start(), calls=%async_computation.11 | async-start | bytes 3932160 | tf_op jit(solution)/shard_map/all_gather | solution.py:41
  15.0 130.1 %all-gather.9.cloned.1.call-start = ((), (), s32[]{:S(2)}) async-start(), calls=%async_computation.8 | async-start | bytes 3932160 | tf_op jit(solution)/shard_map/all_gather | solution.py:41
  15.7 193.1 %all-gather.11.cloned.1.call-start = ((), (), s32[]{:S(2)}) async-start(), calls=%async_computation.9 | async-start | bytes 3932160 | tf_op jit(solution)/shard_map/all_gather | solution.py:41
  16.5 256.0 %all-gather.13.cloned.1.call-start = ((), (), s32[]{:S(2)}) async-start(), calls=%async_computation.10 | async-start | bytes 3932160 | tf_op jit(solution)/shard_map/all_gather | solution.py:41
  17.1 319.1 %reduce-scatter.11.cloned.1.call-start = ((), (), s32[]{:S(2)}) async-start(), calls=%async_computation.7 | async-start | bytes 7077888 | tf_op jit(solution)/shard_map/reduce_scatter | solution.py:47
  107.5 294.0 %reduce-scatter.5.cloned.1.call-start = ((), (), s32[]{:S(2)}) async-start(), calls=%async_computation.4 | async-start | bytes 7077888 | tf_op jit(solution)/shard_map/reduce_scatter | solution.py:47
  171.3 295.4 %reduce-scatter.7.cloned.1.call-start = ((), (), s32[]{:S(2)}) async-start(), calls=%async_computation.5 | async-start | bytes 7077888 | tf_op jit(solution)/shard_map/reduce_scatter | solution.py:47
  235.0 297.2 %reduce-scatter.9.cloned.1.call-start = ((), (), s32[]{:S(2)}) async-start(), calls=%async_computation.6 | async-start | bytes 7077888 | tf_op jit(solution)/shard_map/reduce_scatter | solution.py:47
Sparse Core Ops, SparseCore 0:
  15.1 66.1 all-gather.14
  82.9 62.1 all-gather.8
  146.7 62.1 all-gather.10
  210.3 62.1 all-gather.12
  275.7 60.3 reduce-scatter.10
  339.7 61.7 reduce-scatter.4
  404.9 61.7 reduce-scatter.6
  470.4 61.7 reduce-scatter.8
where the time goes:
time: 543 us
  waiting for transfers between devices  411 us (76%)
  matrix products  105 us (19%)
  between operations  13.5 us (2%)
  local copies, waits for them, and re-layouts  6.92 us (1%)
  other arithmetic  6.4 us (1%)
    reduce_scatter x4, waiting for transfers between devices, local(): sums.append(lax.psum_scatter(part, 'bcol', scatter_dimension=0, tiled=True))  233 us
    all_gather x4, waiting for transfers between devices, local(): lax.all_gather(factor[:, q], 'brow', axis=0, tiled=True)  176 us
    dot_general x4, matrix products, product(): lax.dot_general(x, y, (((1,), (1,)), ((), ())), preferred_element_type=jn...  105 us
  transfers between devices with their start and end apart: 8, of which 8 were waited for; matrix products, arithmetic and copies ran while one was open for 19% of the time, Pallas kernels for 0%

commit v1 on v0

--- a/solution.py
+++ b/solution.py
@@ -8,6 +8,19 @@
 A = 32
 K = 1
 CHUNKS = 4
+
+
+def collect(x, axis, dim):
+    ways = lax.axis_size(axis)
+    up = [(d, (d + 1) % ways) for d in range(ways)]
+    down = [(d, (d - 1) % ways) for d in range(ways)]
+    earlier, later = ([x], [x])
+    for _ in range(ways // 2):
+        earlier.append(lax.ppermute(earlier[-1], axis, up))
+    for _ in range((ways - 1) // 2):
+        later.append(lax.ppermute(later[-1], axis, down))
+    line = jnp.concatenate([*earlier[::-1], *later[1:]], axis=dim)
+    return jnp.roll(line, (lax.axis_index(axis) - ways // 2) * x.shape[dim], axis=dim)
 
 
 def split(x):
@@ -37,10 +50,7 @@
     factor = jnp.where(col_mask, factor_pieces.T, 0.0)
     width = total_cols // n_col // CHUNKS
     factor = factor.reshape(-1, CHUNKS, width, block_cols)
-    gathered = [
-        lax.all_gather(factor[:, q], "brow", axis=0, tiled=True).reshape(-1, block_cols)
-        for q in range(CHUNKS)
-    ]
+    gathered = [collect(factor[:, q], "brow", 0).reshape(-1, block_cols) for q in range(CHUNKS)]
     sums = []
     for q in range(CHUNKS):
         part = product(gathered[q], ancestor_inverse, precision=lax.Precision.HIGH)

time: 543 us -> 410 us (0.76)
  waiting for transfers between devices: 411 us -> 239 us
  starting transfers between devices: 0.68 us -> 31.5 us
  other arithmetic: 6.4 us -> 18.3 us
    ppermute x0 -> x12, waiting for transfers between devices: none -> 180 us  [the longest x8 137 us: collect(): earlier.append(lax.ppermute(earlier[-1], axis, up))]
    all_gather x4 -> x0, waiting for transfers between devices: 176 us -> none  [local(): lax.all_gather(factor[:, q], 'brow', axis=0, tiled=True)]
    reduce_scatter x4, waiting for transfers between devices: 233 us -> 59.2 us  [local(): sums.append(lax.psum_scatter(part, 'bcol', scatter_dimension=0, tiled=True))]
    ppermute x0 -> x12, starting transfers between devices: none -> 31.3 us  [the longest x8 17.8 us: collect(): earlier.append(lax.ppermute(earlier[-1], axis, up))]
    concatenate x0 -> x4, other arithmetic: none -> 11.9 us  [collect(): jnp.roll(line, (lax.axis_index(axis) - ways // 2) * x.shape[dim], axis=dim)]
  transfers between devices with their start and end apart: 8 -> 16, of which waited for: 8 -> 13; matrix products, arithmetic and copies ran while one was open for 19% -> 21% of each run, Pallas kernels for 0% -> 0%
where the time goes in v1:
time: 410 us
  waiting for transfers between devices  239 us (58%)
  matrix products  102 us (25%)
  starting transfers between devices  31.5 us (8%)
  other arithmetic  18.3 us (4%)
  between operations  13.3 us (3%)
  local copies, waits for them, and re-layouts  5.49 us (1%)
    ppermute x8, waiting for transfers between devices, collect(): earlier.append(lax.ppermute(earlier[-1], axis, up))  137 us
    dot_general x4, matrix products, product(): lax.dot_general(x, y, (((1,), (1,)), ((), ())), preferred_element_type=jn...  102 us
    reduce_scatter x4, waiting for transfers between devices, local(): sums.append(lax.psum_scatter(part, 'bcol', scatter_dimension=0, tiled=True))  59.2 us
    ppermute x4, waiting for transfers between devices, collect(): later.append(lax.ppermute(later[-1], axis, down))  43 us
    ppermute x8, starting transfers between devices, collect(): earlier.append(lax.ppermute(earlier[-1], axis, up))  17.8 us
    ppermute x4, starting transfers between devices, collect(): later.append(lax.ppermute(later[-1], axis, down))  13.5 us
    concatenate x4, other arithmetic, collect(): jnp.roll(line, (lax.axis_index(axis) - ways // 2) * x.shape[dim], axis=dim)  11.9 us
  transfers between devices with their start and end apart: 16, of which 13 were waited for; matrix products, arithmetic and copies ran while one was open for 21% of the time, Pallas kernels for 0%

profile of v1, /device:TPU:0, one launch (start us, length us, event | category | flops | bytes accessed | tf_op | source)
XLA Modules:
  0.0 409.5 jit_solution(6713128231130608711)
XLA Ops:
  18.7 18.5 %collective-permute-done = f32[2,48,2048]{2,1,0:T(8,128)} collective-permute-done((f32[2,48,2048]{2,1,0:T(8,128)S(1)}, f32[2,48,2048]{2,1,0:T(8,128)}, u32[]{:S(2)}, u32[]{:S(2)}) %collective-permute-start) | collective-permute-done | bytes 786464 | tf_op jit(solution)/shard_map/ppermute | solution.py:19
  37.2 15.6 %collective-permute-done.2 = f32[2,48,2048]{2,1,0:T(8,128)} collective-permute-done((f32[2,48,2048]{2,1,0:T(8,128)S(1)}, f32[2,48,2048]{2,1,0:T(8,128)}, u32[]{:S(2)}, u32[]{:S(2)}) %collective-permute-start.2) | collective-permute-done | bytes 786464 | tf_op jit(solution)/shard_map/ppermute | solution.py:21
  52.8 17.2 %collective-permute-done.1 = f32[2,48,2048]{2,1,0:T(8,128)} collective-permute-done((f32[2,48,2048]{2,1,0:T(8,128)}, f32[2,48,2048]{2,1,0:T(8,128)}, u32[]{:S(2)}, u32[]{:S(2)}) %collective-permute-start.1) | collective-permute-done | bytes 786464 | tf_op jit(solution)/shard_map/ppermute | solution.py:19
  70.0 3.9 fusion.24
  73.9 25.4 %fusion.30 = f32[384,4096]{1,0:T(8,128)} fusion(f32[384,2048]{1,0:T(8,128)S(1)} %bitcast.29, f32[4096,2048]{1,0:T(8,128)} %param.6), kind=kOutput, calls=%fused_computation.69 | convolution fusion | flops 19327352832 | bytes 42991616 | tf_op jit(solution)/shard_map/dot_general | solution.py:32
  99.4 3.8 collective-permute-start.5
  103.3 18.5 %collective-permute-done.3 = f32[2,48,2048]{2,1,0:T(8,128)S(1)} collective-permute-done((f32[2,48,2048]{2,1,0:T(8,128)S(1)}, f32[2,48,2048]{2,1,0:T(8,128)S(1)}, u32[]{:S(2)}, u32[]{:S(2)}) %collective-permute-start.3) | collective-permute-done | bytes 786464 | tf_op jit(solution)/shard_map/ppermute | solution.py:19
  121.7 15.0 %collective-permute-done.5 = f32[2,48,2048]{2,1,0:T(8,128)S(1)} collective-permute-done((f32[2,48,2048]{2,1,0:T(8,128)S(1)}, f32[2,48,2048]{2,1,0:T(8,128)S(1)}, u32[]{:S(2)}, u32[]{:S(2)}) %collective-permute-start.5) | collective-permute-done | bytes 786464 | tf_op jit(solution)/shard_map/ppermute | solution.py:21
  136.7 15.1 %collective-permute-done.4 = f32[2,48,2048]{2,1,0:T(8,128)S(1)} collective-permute-done((f32[2,48,2048]{2,1,0:T(8,128)S(1)}, f32[2,48,2048]{2,1,0:T(8,128)S(1)}, u32[]{:S(2)}, u32[]{:S(2)}) %collective-permute-start.4) | collective-permute-done | bytes 786464 | tf_op jit(solution)/shard_map/ppermute | solution.py:19
  154.6 25.5 %fusion.31 = f32[384,4096]{1,0:T(8,128)} fusion(f32[384,2048]{1,0:T(8,128)S(1)} %bitcast.30, f32[4096,2048]{1,0:T(8,128)} %param.6), kind=kOutput, calls=%fused_computation.70 | convolution fusion | flops 19327352832 | bytes 42991616 | tf_op jit(solution)/shard_map/dot_general | solution.py:32
  180.2 3.8 collective-permute-start.8
  184.0 18.5 %collective-permute-done.6 = f32[2,48,2048]{2,1,0:T(8,128)S(1)} collective-permute-done((f32[2,48,2048]{2,1,0:T(8,128)S(1)}, f32[2,48,2048]{2,1,0:T(8,128)S(1)}, u32[]{:S(2)}, u32[]{:S(2)}) %collective-permute-start.6) | collective-permute-done | bytes 786464 | tf_op jit(solution)/shard_map/ppermute | solution.py:19
  202.5 6.9 %collective-permute-start.7 = (f32[2,48,2048]{2,1,0:T(8,128)S(1)}, f32[2,48,2048]{2,1,0:T(8,128)S(1)}, u32[]{:S(2)}, u32[]{:S(2)}) collective-permute-start(f32[2,48,2048]{2,1,0:T(8,128)S(1)} %collective-permute-done.6), channel_id=1, source_target_pairs={{0,8},{8,16},{16,24},{24,0},{1,9},{9,17},{17,25},{25,1},{2,10},{10... | collective-permute-start | bytes 2359304 | tf_op jit(solution)/shard_map/ppermute | solution.py:19
  209.4 6.7 %collective-permute-done.8 = f32[2,48,2048]{2,1,0:T(8,128)S(1)} collective-permute-done((f32[2,48,2048]{2,1,0:T(8,128)S(1)}, f32[2,48,2048]{2,1,0:T(8,128)S(1)}, u32[]{:S(2)}, u32[]{:S(2)}) %collective-permute-start.8) | collective-permute-done | bytes 786464 | tf_op jit(solution)/shard_map/ppermute | solution.py:21
  216.1 15.6 %collective-permute-done.7 = f32[2,48,2048]{2,1,0:T(8,128)S(1)} collective-permute-done((f32[2,48,2048]{2,1,0:T(8,128)S(1)}, f32[2,48,2048]{2,1,0:T(8,128)S(1)}, u32[]{:S(2)}, u32[]{:S(2)}) %collective-permute-start.7) | collective-permute-done | bytes 786464 | tf_op jit(solution)/shard_map/ppermute | solution.py:19
  234.4 25.4 %fusion.32 = f32[384,4096]{1,0:T(8,128)} fusion(f32[384,2048]{1,0:T(8,128)S(1)} %bitcast.31, f32[4096,2048]{1,0:T(8,128)} %param.6), kind=kOutput, calls=%fused_computation.71 | convolution fusion | flops 19327352832 | bytes 42991616 | tf_op jit(solution)/shard_map/dot_general | solution.py:32
  260.0 3.8 collective-permute-start.11
  263.8 18.5 %collective-permute-done.9 = f32[2,48,2048]{2,1,0:T(8,128)S(1)} collective-permute-done((f32[2,48,2048]{2,1,0:T(8,128)S(1)}, f32[2,48,2048]{2,1,0:T(8,128)S(1)}, u32[]{:S(2)}, u32[]{:S(2)}) %collective-permute-start.9) | collective-permute-done | bytes 786464 | tf_op jit(solution)/shard_map/ppermute | solution.py:19
  282.3 7.6 %collective-permute-start.10 = (f32[2,48,2048]{2,1,0:T(8,128)S(1)}, f32[2,48,2048]{2,1,0:T(8,128)S(1)}, u32[]{:S(2)}, u32[]{:S(2)}) collective-permute-start(f32[2,48,2048]{2,1,0:T(8,128)S(1)} %collective-permute-done.9), channel_id=1, source_target_pairs={{0,8},{8,16},{16,24},{24,0},{1,9},{9,17},{17,25},{25,1},{2,10},{10... | collective-permute-start | bytes 2359304 | tf_op jit(solution)/shard_map/ppermute | solution.py:19
  289.9 5.7 %collective-permute-done.11 = f32[2,48,2048]{2,1,0:T(8,128)S(1)} collective-permute-done((f32[2,48,2048]{2,1,0:T(8,128)S(1)}, f32[2,48,2048]{2,1,0:T(8,128)S(1)}, u32[]{:S(2)}, u32[]{:S(2)}) %collective-permute-start.11) | collective-permute-done | bytes 786464 | tf_op jit(solution)/shard_map/ppermute | solution.py:21
  295.6 15.0 %collective-permute-done.10 = f32[2,48,2048]{2,1,0:T(8,128)S(1)} collective-permute-done((f32[2,48,2048]{2,1,0:T(8,128)S(1)}, f32[2,48,2048]{2,1,0:T(8,128)S(1)}, u32[]{:S(2)}, u32[]{:S(2)}) %collective-permute-start.10) | collective-permute-done | bytes 786464 | tf_op jit(solution)/shard_map/ppermute | solution.py:19
  313.3 25.5 %fusion.33 = f32[384,4096]{1,0:T(8,128)} fusion(f32[384,2048]{1,0:T(8,128)S(1)} %bitcast.28, f32[4096,2048]{1,0:T(8,128)} %param.6), kind=kOutput, calls=%fused_computation.72 | convolution fusion | flops 19327352832 | bytes 42991616 | tf_op jit(solution)/shard_map/dot_general | solution.py:32
  339.8 59.2 %reduce-scatter.11.cloned.1.call-done = f32[48,4096]{1,0:T(8,128)} async-done(((f32[384,4096]{1,0:T(8,128)}), f32[48,4096]{1,0:T(8,128)}) %reduce-scatter.11.cloned.1.call-update) | async-done | bytes 786448 | tf_op jit(solution)/shard_map/reduce_scatter | solution.py:57
  399.0 4.0 fusion.28
  (31 shorter events, 21.5 us)
Async XLA Ops:
  6.5 333.2 %reduce-scatter.5.cloned.1.call-start = ((), (), s32[]{:S(2)}) async-start(), calls=%async_computation.4 | async-start | bytes 7077888 | tf_op jit(solution)/shard_map/reduce_scatter | solution.py:57
  13.5 23.6 %collective-permute-start = (f32[2,48,2048]{2,1,0:T(8,128)S(1)}, f32[2,48,2048]{2,1,0:T(8,128)}, u32[]{:S(2)}, u32[]{:S(2)}) collective-permute-start(f32[2,48,2048]{2,1,0:T(8,128)S(1)} %get-tuple-element.6), channel_id=1, source_target_pairs={{0,8},{8,16},{16,24},{24,0},{1,9},{9,17},{17,25},{25,1},{2,10},{10... | collective-permute-start | bytes 2359304 | tf_op jit(solution)/shard_map/ppermute | solution.py:19
  16.6 36.2 %collective-permute-start.2 = (f32[2,48,2048]{2,1,0:T(8,128)S(1)}, f32[2,48,2048]{2,1,0:T(8,128)}, u32[]{:S(2)}, u32[]{:S(2)}) collective-permute-start(f32[2,48,2048]{2,1,0:T(8,128)S(1)} %get-tuple-element.6), channel_id=1, source_target_pairs={{0,24},{8,0},{16,8},{24,16},{1,25},{9,1},{17,9},{25,17},{2,26},{10... | collective-permute-start | bytes 2359304 | tf_op jit(solution)/shard_map/ppermute | solution.py:21
  37.2 32.9 %collective-permute-start.1 = (f32[2,48,2048]{2,1,0:T(8,128)}, f32[2,48,2048]{2,1,0:T(8,128)}, u32[]{:S(2)}, u32[]{:S(2)}) collective-permute-start(f32[2,48,2048]{2,1,0:T(8,128)} %collective-permute-done), channel_id=1, source_target_pairs={{0,8},{8,16},{16,24},{24,0},{1,9},{9,17},{17,25},{25,1},{2,10},{10... | collective-permute-start | bytes 2359304 | tf_op jit(solution)/shard_map/ppermute | solution.py:19
  99.3 240.4 %reduce-scatter.7.cloned.1.call-start = ((), (), s32[]{:S(2)}) async-start(), calls=%async_computation.5 | async-start | bytes 7077888 | tf_op jit(solution)/shard_map/reduce_scatter | solution.py:57
  99.4 22.3 %collective-permute-start.3 = (f32[2,48,2048]{2,1,0:T(8,128)S(1)}, f32[2,48,2048]{2,1,0:T(8,128)S(1)}, u32[]{:S(2)}, u32[]{:S(2)}) collective-permute-start(f32[2,48,2048]{2,1,0:T(8,128)S(1)} %get-tuple-element.9), channel_id=1, source_target_pairs={{0,8},{8,16},{16,24},{24,0},{1,9},{9,17},{17,25},{25,1},{2,10},{10... | collective-permute-start | bytes 2359304 | tf_op jit(solution)/shard_map/ppermute | solution.py:19
  99.4 37.3 %collective-permute-start.5 = (f32[2,48,2048]{2,1,0:T(8,128)S(1)}, f32[2,48,2048]{2,1,0:T(8,128)S(1)}, u32[]{:S(2)}, u32[]{:S(2)}) collective-permute-start(f32[2,48,2048]{2,1,0:T(8,128)S(1)} %get-tuple-element.9), channel_id=1, source_target_pairs={{0,24},{8,0},{16,8},{24,16},{1,25},{9,1},{17,9},{25,17},{2,26},{10... | collective-permute-start | bytes 2359304 | tf_op jit(solution)/shard_map/ppermute | solution.py:21
  121.7 30.2 %collective-permute-start.4 = (f32[2,48,2048]{2,1,0:T(8,128)S(1)}, f32[2,48,2048]{2,1,0:T(8,128)S(1)}, u32[]{:S(2)}, u32[]{:S(2)}) collective-permute-start(f32[2,48,2048]{2,1,0:T(8,128)S(1)} %collective-permute-done.3), channel_id=1, source_target_pairs={{0,8},{8,16},{16,24},{24,0},{1,9},{9,17},{17,25},{25,1},{2,10},{10... | collective-permute-start | bytes 2359304 | tf_op jit(solution)/shard_map/ppermute | solution.py:19
  180.1 159.7 %reduce-scatter.9.cloned.1.call-start = ((), (), s32[]{:S(2)}) async-start(), calls=%async_computation.6 | async-start | bytes 7077888 | tf_op jit(solution)/shard_map/reduce_scatter | solution.py:57
  180.1 22.3 %collective-permute-start.6 = (f32[2,48,2048]{2,1,0:T(8,128)S(1)}, f32[2,48,2048]{2,1,0:T(8,128)S(1)}, u32[]{:S(2)}, u32[]{:S(2)}) collective-permute-start(f32[2,48,2048]{2,1,0:T(8,128)S(1)} %get-tuple-element.8), channel_id=1, source_target_pairs={{0,8},{8,16},{16,24},{24,0},{1,9},{9,17},{17,25},{25,1},{2,10},{10... | collective-permute-start | bytes 2359304 | tf_op jit(solution)/shard_map/ppermute | solution.py:19
  180.2 35.9 %collective-permute-start.8 = (f32[2,48,2048]{2,1,0:T(8,128)S(1)}, f32[2,48,2048]{2,1,0:T(8,128)S(1)}, u32[]{:S(2)}, u32[]{:S(2)}) collective-permute-start(f32[2,48,2048]{2,1,0:T(8,128)S(1)} %get-tuple-element.8), channel_id=1, source_target_pairs={{0,24},{8,0},{16,8},{24,16},{1,25},{9,1},{17,9},{25,17},{2,26},{10... | collective-permute-start | bytes 2359304 | tf_op jit(solution)/shard_map/ppermute | solution.py:21
  202.5 29.3 %collective-permute-start.7 = (f32[2,48,2048]{2,1,0:T(8,128)S(1)}, f32[2,48,2048]{2,1,0:T(8,128)S(1)}, u32[]{:S(2)}, u32[]{:S(2)}) collective-permute-start(f32[2,48,2048]{2,1,0:T(8,128)S(1)} %collective-permute-done.6), channel_id=1, source_target_pairs={{0,8},{8,16},{16,24},{24,0},{1,9},{9,17},{17,25},{25,1},{2,10},{10... | collective-permute-start | bytes 2359304 | tf_op jit(solution)/shard_map/ppermute | solution.py:19
  259.9 139.1 %reduce-scatter.11.cloned.1.call-start = ((), (), s32[]{:S(2)}) async-start(), calls=%async_computation.7 | async-start | bytes 7077888 | tf_op jit(solution)/shard_map/reduce_scatter | solution.py:57
  260.0 22.3 %collective-permute-start.9 = (f32[2,48,2048]{2,1,0:T(8,128)S(1)}, f32[2,48,2048]{2,1,0:T(8,128)S(1)}, u32[]{:S(2)}, u32[]{:S(2)}) collective-permute-start(f32[2,48,2048]{2,1,0:T(8,128)S(1)} %get-tuple-element.7), channel_id=1, source_target_pairs={{0,8},{8,16},{16,24},{24,0},{1,9},{9,17},{17,25},{25,1},{2,10},{10... | collective-permute-start | bytes 2359304 | tf_op jit(solution)/shard_map/ppermute | solution.py:19
  260.0 35.6 %collective-permute-start.11 = (f32[2,48,2048]{2,1,0:T(8,128)S(1)}, f32[2,48,2048]{2,1,0:T(8,128)S(1)}, u32[]{:S(2)}, u32[]{:S(2)}) collective-permute-start(f32[2,48,2048]{2,1,0:T(8,128)S(1)} %get-tuple-element.7), channel_id=1, source_target_pairs={{0,24},{8,0},{16,8},{24,16},{1,25},{9,1},{17,9},{25,17},{2,26},{10... | collective-permute-start | bytes 2359304 | tf_op jit(solution)/shard_map/ppermute | solution.py:21
  282.3 28.3 %collective-permute-start.10 = (f32[2,48,2048]{2,1,0:T(8,128)S(1)}, f32[2,48,2048]{2,1,0:T(8,128)S(1)}, u32[]{:S(2)}, u32[]{:S(2)}) collective-permute-start(f32[2,48,2048]{2,1,0:T(8,128)S(1)} %collective-permute-done.9), channel_id=1, source_target_pairs={{0,8},{8,16},{16,24},{24,0},{1,9},{9,17},{17,25},{25,1},{2,10},{10... | collective-permute-start | bytes 2359304 | tf_op jit(solution)/shard_map/ppermute | solution.py:19
Sparse Core Ops, SparseCore 0:
  99.4 61.0 reduce-scatter.4
  180.2 59.9 reduce-scatter.6
  260.0 59.9 reduce-scatter.8
  338.9 59.9 reduce-scatter.10
